TPU v7x, 32 devices: a whole 2x2x4 slice. The times are simulated.
32 devices in a mesh: grp: 4 (over x, core), mem: 8 (over z, y).
Axes of the slice: x: 2, y: 2, z: 4, core: 2. Of those that a mesh axis runs over, the one named last changes fastest.
Arguments:
- features: bfloat16 [32768, 4096], P(('grp', 'mem')), may hold values from -0.09375 to 0.09375
- re_features: bfloat16 [32768, 256], P(('grp', 'mem')), may hold values from -6 to 6
- member_id: int32 [32768], P(('grp', 'mem')), may hold values from 0 to 255, as said below
- slot: int32 [32768], P(('grp', 'mem')), may hold values from 0 to 2047, as said below
- labels: int32 [32768], P(('grp', 'mem')), may hold values 0 or 1
- offsets: float32 [32768], P(('grp', 'mem')), may hold values from -6 to 6
- feature_scale: float32 [4096], replicated, may hold values from 0.3 to 3
- w_start: float32 [4096], replicated, may hold values from -4 to 4
Outputs:
- fixed_weights: float32 [4096], replicated
- member_coef: float32 [256, 256], P(('grp', 'mem'))
- row_offsets: float32 [32768], P(('grp', 'mem'))
Inputs may be any that keep to these rules, and one draw needn't show every extreme that they name: A row of device k (devices counted along grp, then mem) belongs to group k // 8: member_id // 64 is that group, and (member_id mod 64) // 8 equals slot // 256. Rows per member are uneven. Within one device's rows the slots are distinct; slot // 256 is the mem index that owns the row's member, so at most 256 rows of one device go to one owner, and in every group one owner receives exactly 256 rows from every device of the group.
All inputs are finite; a program needn't handle non-finite values. No bound on the sum of `labels` on one device may be relied on, other than what follows from the above.
Results may differ from a plain program's by a relative error of at most 0.0003.
Values may be sent and summed in bfloat16 or wider, within the bound.
A program may use at most 64 MiB of HBM per device.

v0:
```python
import jax
import jax.numpy as jnp
from jax import lax
from jax.sharding import PartitionSpec as P

MEM_DEV = 8
NEWTON = 2
CG_ITERS = 3
ridge_fixed = 1.0
ridge_member = 1.0


def split_pair(values):
    upper_part = values.astype(jnp.bfloat16)
    held_part = lax.optimization_barrier(upper_part)
    lower_part = (values - held_part.astype(jnp.float32)).astype(jnp.bfloat16)
    return (upper_part, lower_part)


def split_two(vector):
    upper_part, lower_part = split_pair(vector)
    return jnp.stack([upper_part, lower_part], axis=1)


def apply_rows(features, vector):
    return jnp.sum(jnp.dot(features, split_two(vector), preferred_element_type=jnp.float32), axis=1)


def apply_columns(features, values):
    pair_cols = split_two(values)
    product = lax.dot_general(
        pair_cols, features, (((0,), (0,)), ((), ())), preferred_element_type=jnp.float32
    )
    return jnp.sum(product, axis=0)


def inner_rows(left, right):
    return lax.dot_general(
        left, right, (((0,), (0,)), ((), ())), preferred_element_type=jnp.float32
    )


def hessian_times(features, feature_scale, curvature, direction):
    inner = curvature * apply_rows(features, feature_scale * direction)
    summed = lax.psum(apply_columns(features, inner), ("grp", "mem"))
    return feature_scale * summed + ridge_fixed * direction


def fit_members(received, arrived):
    curv_row = arrived[0]
    resid_row = arrived[1]
    local_row = arrived[2]
    onehot = (local_row[:, None] == jnp.arange(MEM_DEV).astype(arrived.dtype)[None, :]).astype(
        arrived.dtype
    )
    z_float = received.astype(jnp.float32)

    def gram_one(column):
        upper_part, lower_part = split_pair(z_float * (curv_row * column)[:, None])
        return inner_rows(received, upper_part) + inner_rows(received, lower_part)

    gram_all = lax.map(gram_one, onehot.T) + ridge_member * jnp.eye(
        received.shape[1], dtype=jnp.float32
    )
    grad_upper, grad_lower = split_pair(resid_row[:, None] * onehot)
    member_grad = inner_rows(grad_upper, received) + inner_rows(grad_lower, received)
    factor = jnp.linalg.cholesky(gram_all)
    member_coef = -jax.scipy.linalg.cho_solve((factor, True), member_grad[:, :, None])[:, :, 0]
    coef_upper, coef_lower = split_pair(member_coef)
    scores = jnp.dot(received, coef_upper.T, preferred_element_type=jnp.float32) + jnp.dot(
        received, coef_lower.T, preferred_element_type=jnp.float32
    )
    return (member_coef, jnp.sum(scores * onehot, axis=1))


def on_device(features, re_features, member_id, slot, labels, offsets, feature_scale, w_start):
    row_count = features.shape[0]
    slots_all = 2 * row_count
    packed = jnp.zeros((slots_all, re_features.shape[1]), jnp.bfloat16).at[slot].set(re_features)
    received = None
    target = labels.astype(jnp.float32)
    weights = w_start
    for newton_step in range(NEWTON):
        margin = apply_rows(features, feature_scale * weights) + offsets
        probability = jax.nn.sigmoid(margin)
        curvature = probability * (1.0 - probability)
        summed = lax.psum(apply_columns(features, probability - target), ("grp", "mem"))
        gradient = feature_scale * summed + ridge_fixed * weights
        residual = -gradient
        direction = residual
        res_norm = jnp.sum(residual * residual)
        update = jnp.zeros_like(weights)
        for cg_step in range(CG_ITERS):
            hess_image = hessian_times(features, feature_scale, curvature, direction)
            step_size = res_norm / jnp.sum(direction * hess_image)
            update = update + step_size * direction
            residual = residual - step_size * hess_image
            next_norm = jnp.sum(residual * residual)
            direction = residual + next_norm / res_norm * direction
            res_norm = next_norm
        weights = weights + update
    score = apply_rows(features, feature_scale * weights)
    probability = jax.nn.sigmoid(score)
    curvature = probability * (1.0 - probability)
    resid_row = probability - target
    local_id = (member_id % MEM_DEV).astype(jnp.float32)
    row_weights = jnp.stack([curvature, resid_row, local_id], axis=0)
    weight_slots = jnp.zeros((3, slots_all), jnp.float32).at[:, slot].set(row_weights)
    received = lax.all_to_all(packed, "mem", split_axis=0, concat_axis=0, tiled=True)
    arrived = lax.all_to_all(weight_slots, "mem", split_axis=1, concat_axis=1, tiled=True)
    member_coef, slot_scores = fit_members(received, arrived)
    returned = lax.all_to_all(slot_scores, "mem", split_axis=0, concat_axis=0, tiled=True)
    row_offsets = returned[slot]
    return (weights, member_coef, row_offsets)


def solution(mesh):
    placed = (
        P(("grp", "mem"), None),
        P(("grp", "mem"), None),
        P(("grp", "mem")),
        P(("grp", "mem")),
        P(("grp", "mem")),
        P(("grp", "mem")),
        P(),
        P(),
    )
    return jax.shard_map(
        on_device,
        mesh=mesh,
        in_specs=placed,
        out_specs=(P(), P(("grp", "mem"), None), P(("grp", "mem"))),
        check_vma=False,
    )
```

profile of v0, /device:TPU:0, one launch (start us, length us, event | category | flops | bytes accessed | tf_op | source)
XLA Modules:
  0.0 981.4 jit_solution(12740496581098813807)
XLA Ops:
  1.5 5.8 convolution_reduce_fusion.16
  8.6 42.1 %psum.56 = f32[4096]{0:T(1024)S(1)} all-reduce(f32[4096]{0:T(1024)S(1)} %convolution_reduce_fusion.7), channel_id=1, replica_groups=mesh['grp'=4,'mem'=8] {'grp','mem'}, use_global_device_ids=true, to_apply=%region_2.0 | all-reduce | flops 4096 | bytes 32768 | tf_op jit(solution)/shard_map/psum | solution.py:87
  50.8 5.8 convolution_reduce_fusion.15
  57.9 40.2 %psum.57 = f32[4096]{0:T(1024)S(1)} all-reduce(f32[4096]{0:T(1024)S(1)} %convolution_reduce_fusion.6), channel_id=1, replica_groups=mesh['grp'=4,'mem'=8] {'grp','mem'}, use_global_device_ids=true, to_apply=%region_6.0 | all-reduce | flops 4096 | bytes 32768 | tf_op jit(solution)/shard_map/psum | solution.py:45
  102.1 5.7 convolution_reduce_fusion.14
  107.8 4.6 convolution_reduce_fusion.5
  112.4 40.2 %psum.58 = f32[4096]{0:T(1024)S(1)} all-reduce(f32[4096]{0:T(1024)S(1)} %convolution_reduce_fusion.5), channel_id=1, replica_groups=mesh['grp'=4,'mem'=8] {'grp','mem'}, use_global_device_ids=true, to_apply=%region_11.0 | all-reduce | flops 4096 | bytes 32768 | tf_op jit(solution)/shard_map/psum | solution.py:45
  156.6 5.7 convolution_reduce_fusion.13
  162.3 4.6 convolution_reduce_fusion.4
  166.9 40.2 %psum.59 = f32[4096]{0:T(1024)S(1)} all-reduce(f32[4096]{0:T(1024)S(1)} %convolution_reduce_fusion.4), channel_id=1, replica_groups=mesh['grp'=4,'mem'=8] {'grp','mem'}, use_global_device_ids=true, to_apply=%region_16.0 | all-reduce | flops 4096 | bytes 32768 | tf_op jit(solution)/shard_map/psum | solution.py:45
  209.1 5.7 convolution_reduce_fusion.12
  214.9 4.6 convolution_reduce_fusion.3
  219.5 40.1 %psum.60 = f32[4096]{0:T(1024)S(1)} all-reduce(f32[4096]{0:T(1024)S(1)} %convolution_reduce_fusion.3), channel_id=1, replica_groups=mesh['grp'=4,'mem'=8] {'grp','mem'}, use_global_device_ids=true, to_apply=%region_20.0 | all-reduce | flops 4096 | bytes 32768 | tf_op jit(solution)/shard_map/psum | solution.py:87
  259.6 5.7 convolution_reduce_fusion.11
  265.3 4.6 convolution_reduce_fusion.2
  269.9 40.7 %psum.61 = f32[4096]{0:T(1024)S(1)} all-reduce(f32[4096]{0:T(1024)S(1)} %convolution_reduce_fusion.2), channel_id=1, replica_groups=mesh['grp'=4,'mem'=8] {'grp','mem'}, use_global_device_ids=true, to_apply=%region_24.0 | all-reduce | flops 4096 | bytes 32768 | tf_op jit(solution)/shard_map/psum | solution.py:45
  314.5 5.7 convolution_reduce_fusion.10
  320.3 4.6 convolution_reduce_fusion.1
  324.8 39.9 %psum.62 = f32[4096]{0:T(1024)S(1)} all-reduce(f32[4096]{0:T(1024)S(1)} %convolution_reduce_fusion.1), channel_id=1, replica_groups=mesh['grp'=4,'mem'=8] {'grp','mem'}, use_global_device_ids=true, to_apply=%region_29.0 | all-reduce | flops 4096 | bytes 32768 | tf_op jit(solution)/shard_map/psum | solution.py:45
  368.7 5.7 convolution_reduce_fusion.9
  374.5 4.6 convolution_reduce_fusion
  379.1 40.3 %psum.63 = f32[4096]{0:T(1024)S(1)} all-reduce(f32[4096]{0:T(1024)S(1)} %convolution_reduce_fusion), channel_id=1, replica_groups=mesh['grp'=4,'mem'=8] {'grp','mem'}, use_global_device_ids=true, to_apply=%region_34.0 | all-reduce | flops 4096 | bytes 32768 | tf_op jit(solution)/shard_map/psum | solution.py:45
  422.6 5.7 convolution_reduce_fusion.8
  428.6 3.5 scatter_custom_fusion
  433.0 5.2 all-to-all-start
  438.2 6.4 scatter_custom_fusion.1
  444.9 5.7 all-to-all-start.1
  453.3 22.0 %all-to-all-done.1 = bf16[8,256,256]{2,1,0:T(8,128)(2,1)S(1)} async-done(((bf16[8,256,256]{2,1,0:T(8,128)(2,1)}), bf16[8,256,256]{2,1,0:T(8,128)(2,1)S(1)}, u32[]{:S(2)}, u32[]{:S(2)}) %all-to-all-start.1) | async-done | bytes 1048608 | tf_op jit(solution)/shard_map/all_to_all | solution.py:109
  476.4 19.9 %while.11 = (s32[]{:T(128)}, f32[8,256,256]{1,2,0:T(8,128)}, f32[8,2048]{1,0:T(8,128)S(1)}, f32[2048]{0:T(1024)S(1)}, f32[2048,256]{1,0:T(8,128)S(1)}, /*index=5*/bf16[2048,256]{1,0:T(8,128)(2,1)S(1)}, s32[]{:T(128)}) while((s32[]{:T(128)}, f32[8,256,256]{1,2,0:T(8,128)}, f32[8,2048]{1,0:T(8,128)S(1)}, f32[2048]{0:T(1024)S(1)}, ...), condition=%wide.region_40.41_spmd, body=%wide.region_39.40_spmd.sunk | while | flops 540084224 | bytes 10281053 | solution.py:62
  487.2 1.6 fusion.185
  489.7 1.6 fusion.185
  496.3 3.1 broadcast_add_fusion
  499.4 3.0 copy.34
  502.4 1.9 fusion.4
  505.7 94.4 %custom-call.20 = f32[8,128,128]{2,1,0:T(8,128)} custom-call(f32[8,128,128]{2,1,0:T(8,128)S(1)} %cholesky.119), custom_call_target="Cholesky" | custom-call | tf_op jit(solution)/shard_map/jit(cholesky)/cholesky | solution.py:67
  602.3 80.0 %custom-call.21 = f32[8,1,128,128]{2,3,1,0:T(8,128)} custom-call(f32[8,1,128,128]{3,2,1,0:T(8,128)} %select_bitcast_fusion), custom_call_target="InvertDiagBlocksLowerTriangular" | custom-call | tf_op jit(solution)/shard_map/jit(cholesky)/cholesky | solution.py:67
  682.4 1.9 constant_dynamic-update-slice_fusion.1
  684.3 3.1 convolution_subtract_fusion
  687.3 95.4 %custom-call.22 = f32[8,128,128]{2,1,0:T(8,128)} custom-call(f32[8,128,128]{2,1,0:T(8,128)} %convolution_subtract_fusion), custom_call_target="Cholesky" | custom-call | tf_op jit(solution)/shard_map/jit(cholesky)/cholesky | solution.py:67
  785.7 1.9 select_select_fusion
  787.8 5.9 while.12
  788.4 2.3 bitcast_dynamic-update-slice_fusion.2
  791.4 2.3 bitcast_dynamic-update-slice_fusion.2
  793.7 158.7 %custom-call.23 = f32[8,2,128,128]{2,3,1,0:T(8,128)} custom-call(f32[8,2,128,128]{3,2,1,0:T(8,128)} %bitcast.163), custom_call_target="InvertDiagBlocksLowerTriangular" | custom-call | tf_op jit(solution)/shard_map/jit(_cho_solve)/vmap()/triangular_solve | solution.py:68
  952.4 1.7 fusion.15
  956.6 2.0 fusion.16
  960.9 9.7 all_to_all.33
  970.6 10.5 %gather_fusion = f32[1024]{0:T(1024)} fusion(f32[2048]{0:T(1024)S(1)} %bitcast.135, s32[1024]{0:T(1024)S(1)} %copy-done.20), kind=kCustom, calls=%fused_computation | custom fusion | bytes 12288 | tf_op jit(solution)/shard_map/gather | solution.py:113
  (214 shorter events, 45.4 us)
Async XLA Ops:
  1.4 5.9 copy-start.12
  1.4 5.9 copy-start.19
  1.4 5.9 copy-start
  7.4 43.3 %copy-start.4 = (f32[4096]{0:T(1024)S(1)}, f32[4096]{0:T(1024)}, u32[]{:S(2)}) copy-start(f32[4096]{0:T(1024)} %param.16) | copy-start | bytes 49156
  7.4 43.3 %copy-start.8 = (f32[4096]{0:T(1024)S(1)}, f32[4096]{0:T(1024)}, u32[]{:S(2)}) copy-start(f32[4096]{0:T(1024)} %param.17) | copy-start | bytes 49156
  50.8 5.9 copy-start.1
  374.5 47.5 %copy-start.23 = (s32[1024]{0:T(1024)S(1)}, s32[1024]{0:T(1024)}, u32[]{:S(2)}) copy-start(s32[1024]{0:T(1024)} %param.13) | copy-start | bytes 12292
  374.5 48.1 %copy-start.24 = (s32[1024]{0:T(1024)S(1)}, s32[1024]{0:T(1024)}, u32[]{:S(2)}) copy-start(s32[1024]{0:T(1024)} %param.12) | copy-start | bytes 12292
  433.0 11.9 %all-to-all-start = ((f32[3,8,256]{2,0,1:T(4,128)}), f32[3,8,256]{2,0,1:T(4,128)S(1)}, u32[]{:S(2)}, u32[]{:S(2)}) async-start(f32[3,8,256]{2,0,1:T(4,128)} %copy.32), calls=%async_computation | async-start | bytes 65536 | tf_op jit(solution)/shard_map/all_to_all | solution.py:110
  444.9 30.4 %all-to-all-start.1 = ((bf16[8,256,256]{2,1,0:T(8,128)(2,1)}), bf16[8,256,256]{2,1,0:T(8,128)(2,1)S(1)}, u32[]{:S(2)}, u32[]{:S(2)}) async-start(bf16[8,256,256]{2,1,0:T(8,128)(2,1)} %bitcast.10), calls=%async_computation.1 | async-start | bytes 2097152 | tf_op jit(solution)/shard_map/all_to_all | solution.py:109
  450.7 24.6 %copy-start.21 = (f32[8]{0:T(128)}, f32[8]{0:T(128)S(1)}, u32[]{:S(2)}) copy-start(f32[8]{0:T(128)S(1)} %iota_convert_fusion) | copy-start | bytes 100
  452.5 22.8 %copy-start.9 = (f32[1,8,256]{2,0,1:T(1,128)}, f32[1,8,256]{2,0,1:T(1,128)S(1)}, u32[]{:S(2)}) copy-start(f32[1,8,256]{2,0,1:T(1,128)S(1)} %get-tuple-element.123) | copy-start | bytes 24580
  499.4 3.0 copy-start.2
  504.3 1.4 copy-start.5
  505.7 95.8 %copy-start.14 = (pred[128,128]{1,0:T(8,128)(4,1)S(1)}, pred[128,128]{1,0:T(8,128)(4,1)}, u32[]{:S(2)}) copy-start(pred[128,128]{1,0:T(8,128)(4,1)} %iota_compare_fusion.2) | copy-start | bytes 49156
  600.2 1.3 copy-start.6
  682.4 100.4 %copy-start.10 = (f32[1,8,256]{2,0,1:T(1,128)S(1)}, f32[1,8,256]{2,0,1:T(1,128)}, u32[]{:S(2)}) copy-start(f32[1,8,256]{2,0,1:T(1,128)} %copy-done.9) | copy-start | bytes 24580
  682.4 100.4 %copy-start.11 = (bf16[2048,8]{0,1:T(8,128)(2,1)S(1)}, bf16[2048,8]{0,1:T(8,128)(2,1)}, u32[]{:S(2)}) copy-start(bf16[2048,8]{0,1:T(8,128)(2,1)} %select_convert_fusion) | copy-start | bytes 98308
  682.4 100.4 %copy-start.15 = (f32[8,256]{1,0:T(8,128)S(1)}, f32[8,256]{1,0:T(8,128)}, u32[]{:S(2)}) copy-start(f32[8,256]{1,0:T(8,128)} %fusion.128) | copy-start | bytes 24580
  682.4 100.4 %copy-start.22 = (f32[8]{0:T(128)S(1)}, f32[8]{0:T(128)}, u32[]{:S(2)}) copy-start(f32[8]{0:T(128)} %copy-done.21) | copy-start | bytes 100
  684.3 98.8 %copy-start.13 = (pred[128,128]{1,0:T(8,128)(4,1)S(1)}, pred[128,128]{1,0:T(8,128)(4,1)}, u32[]{:S(2)}) copy-start(pred[128,128]{1,0:T(8,128)(4,1)} %iota_compare_fusion.3) | copy-start | bytes 49156
  783.1 4.6 copy-start.16
  784.4 1.4 copy-start.3
  785.7 1.9 copy-start.25
  787.8 164.6 %slice-start = ((f32[8,256,1]{1,0,2:T(8,128)}), f32[8,128,1]{1,0,2:T(8,128)S(1)}, s32[]{:S(2)}) async-start(f32[8,256,1]{1,0,2:T(8,128)} %copy-done.16), calls=%async_computation.3 | async-start | bytes 8192 | tf_op jit(solution)/shard_map/jit(_cho_solve)/vmap()/triangular_solve | solution.py:68
  787.8 167.2 %copy-start.17 = (f32[8,256,1]{1,0,2:T(8,128)S(1)}, f32[8,256,1]{1,0,2:T(8,128)}, u32[]{:S(2)}) copy-start(f32[8,256,1]{1,0,2:T(8,128)} %copy-done.16) | copy-start | bytes 24580
  952.4 6.8 copy-start.7
  956.6 14.0 %copy-start.20 = (s32[1024]{0:T(1024)S(1)}, s32[1024]{0:T(1024)}, u32[]{:S(2)}) copy-start(s32[1024]{0:T(1024)} %get-tuple-element.126) | copy-start | bytes 12292
  960.1 21.1 %copy-start.18 = (f32[8,256]{1,0:T(8,128)}, f32[8,256]{1,0:T(8,128)S(1)}, u32[]{:S(2)}) copy-start(f32[8,256]{1,0:T(8,128)S(1)} %get-tuple-element.95) | copy-start | bytes 24580
where the time goes:
time: 991 us; the launch traced here: 981 us
  other arithmetic  452 us (46%)
  blocking collectives  333 us (34%)
  matrix products  113 us (11%)
  local copies, waits for them, and re-layouts  35 us (4%)
  waiting for transfers between devices  22.3 us (2%)
  between operations  15.2 us (2%)
  starting transfers between devices  10.9 us (1%)
    another operation x9, other arithmetic, fit_members(): factor = jnp.linalg.cholesky(gram_all)  273 us
    psum x6, blocking collectives, hessian_times(): summed = lax.psum(apply_columns(features, inner), ('grp', 'mem'))  241 us
    another operation x6, other arithmetic, fit_members(): jax.scipy.linalg.cho_solve((factor, True), member_grad[:, :, None])[:, :, 0]  161 us
    psum x2, blocking collectives, on_device(): lax.psum(apply_columns(features, probability - target), ('grp', 'mem'))  82.1 us
    dot_general x9, matrix products, apply_rows(): jnp.dot(features, split_two(vector), preferred_element_type=jnp.float32)  51.3 us
    dot_general x8, matrix products, apply_columns(): lax.dot_general(pair_cols, features, (((0,), (0,)), ((), ())), preferred_...  29.9 us
    all_to_all x1, waiting for transfers between devices, on_device(): lax.all_to_all(packed, 'mem', split_axis=0, concat_axis=0, tiled=True)  22 us
  transfers between devices with their start and end apart: 2, of which 2 were waited for; matrix products, arithmetic and copies ran while one was open for 1% of the time, Pallas kernels for 0%

commit v1 on v0

--- a/solution.py
+++ b/solution.py
@@ -42,7 +42,7 @@
 
 def hessian_times(features, feature_scale, curvature, direction):
     inner = curvature * apply_rows(features, feature_scale * direction)
-    summed = lax.psum(apply_columns(features, inner), ("grp", "mem"))
+    summed = jnp.sum(lax.all_gather(apply_columns(features, inner), ("grp", "mem")), axis=0)
     return feature_scale * summed + ridge_fixed * direction
 
 

time: 991 us -> 1150 us (1.16)
  blocking collectives: 333 us -> 498 us
    all_gather x0 -> x6, blocking collectives: none -> 409 us  [hessian_times(): lax.all_gather(apply_columns(features, inner), ('grp', 'mem'))]
    psum x6 -> x0, blocking collectives: 241 us -> none  [hessian_times(): summed = lax.psum(apply_columns(features, inner), ('grp', 'mem'))]
where the time goes in v1:
time: 1150 us; the launch traced here: 1140 us
  blocking collectives  498 us (43%)
  other arithmetic  452 us (39%)
  matrix products  113 us (10%)
  local copies, waits for them, and re-layouts  35.4 us (3%)
  waiting for transfers between devices  20.8 us (2%)
  between operations  15.2 us (1%)
    all_gather x6, blocking collectives, hessian_times(): lax.all_gather(apply_columns(features, inner), ('grp', 'mem'))  409 us
    another operation x9, other arithmetic, fit_members(): factor = jnp.linalg.cholesky(gram_all)  273 us
    another operation x6, other arithmetic, fit_members(): jax.scipy.linalg.cho_solve((factor, True), member_grad[:, :, None])[:, :, 0]  161 us
    psum x2, blocking collectives, on_device(): lax.psum(apply_columns(features, probability - target), ('grp', 'mem'))  79 us
    dot_general x9, matrix products, apply_rows(): jnp.dot(features, split_two(vector), preferred_element_type=jnp.float32)  51.3 us
    dot_general x8, matrix products, apply_columns(): lax.dot_general(pair_cols, features, (((0,), (0,)), ((), ())), preferred_...  29.9 us
  transfers between devices with their start and end apart: 2, of which 2 were waited for; matrix products, arithmetic and copies ran while one was open for 1% of the time, Pallas kernels for 0%

profile of v1, /device:TPU:0, one launch (start us, length us, event | category | flops | bytes accessed | tf_op | source)
XLA Modules:
  0.0 1144.0 jit_solution(18255535297157110058)
XLA Ops:
  1.5 5.8 convolution_reduce_fusion.16
  8.6 42.1 %psum.14 = f32[4096]{0:T(1024)S(1)} all-reduce(f32[4096]{0:T(1024)S(1)} %convolution_reduce_fusion.7), channel_id=1, replica_groups=mesh['grp'=4,'mem'=8] {'grp','mem'}, use_global_device_ids=true, to_apply=%region_2.0 | all-reduce | flops 4096 | bytes 32768 | tf_op jit(solution)/shard_map/psum | solution.py:87
  50.8 5.8 convolution_reduce_fusion.15
  57.9 69.0 %all-gather = f32[131072]{0:T(1024)S(1)} all-gather(f32[4096]{0:T(1024)S(1)} %convolution_reduce_fusion.6), channel_id=2, replica_groups=mesh['grp'=4,'mem'=8] {'grp','mem'}, dimensions={0}, use_global_device_ids=true | all-gather | bytes 540672 | tf_op jit(solution)/shard_map/all_gather | solution.py:45
  131.0 5.7 convolution_reduce_fusion.14
  136.7 4.6 convolution_reduce_fusion.5
  141.3 66.8 %all-gather.1 = f32[131072]{0:T(1024)S(1)} all-gather(f32[4096]{0:T(1024)S(1)} %convolution_reduce_fusion.5), channel_id=3, replica_groups=mesh['grp'=4,'mem'=8] {'grp','mem'}, dimensions={0}, use_global_device_ids=true | all-gather | bytes 540672 | tf_op jit(solution)/shard_map/all_gather | solution.py:45
  212.3 5.7 convolution_reduce_fusion.13
  218.0 4.6 convolution_reduce_fusion.4
  222.6 69.2 %all-gather.2 = f32[131072]{0:T(1024)S(1)} all-gather(f32[4096]{0:T(1024)S(1)} %convolution_reduce_fusion.4), channel_id=4, replica_groups=mesh['grp'=4,'mem'=8] {'grp','mem'}, dimensions={0}, use_global_device_ids=true | all-gather | bytes 540672 | tf_op jit(solution)/shard_map/all_gather | solution.py:45
  294.0 5.7 convolution_reduce_fusion.12
  299.7 4.6 convolution_reduce_fusion.3
  304.3 36.9 %psum.15 = f32[4096]{0:T(1024)S(1)} all-reduce(f32[4096]{0:T(1024)S(1)} %convolution_reduce_fusion.3), channel_id=1, replica_groups=mesh['grp'=4,'mem'=8] {'grp','mem'}, use_global_device_ids=true, to_apply=%region_20.0 | all-reduce | flops 4096 | bytes 32768 | tf_op jit(solution)/shard_map/psum | solution.py:87
  341.3 5.7 convolution_reduce_fusion.11
  347.0 4.6 convolution_reduce_fusion.2
  351.6 69.3 %all-gather.3 = f32[131072]{0:T(1024)S(1)} all-gather(f32[4096]{0:T(1024)S(1)} %convolution_reduce_fusion.2), channel_id=5, replica_groups=mesh['grp'=4,'mem'=8] {'grp','mem'}, dimensions={0}, use_global_device_ids=true | all-gather | bytes 540672 | tf_op jit(solution)/shard_map/all_gather | solution.py:45
  425.1 5.7 convolution_reduce_fusion.10
  430.8 4.6 convolution_reduce_fusion.1
  435.4 66.6 %all-gather.4 = f32[131072]{0:T(1024)S(1)} all-gather(f32[4096]{0:T(1024)S(1)} %convolution_reduce_fusion.1), channel_id=6, replica_groups=mesh['grp'=4,'mem'=8] {'grp','mem'}, dimensions={0}, use_global_device_ids=true | all-gather | bytes 540672 | tf_op jit(solution)/shard_map/all_gather | solution.py:45
  506.1 5.7 convolution_reduce_fusion.9
  511.9 4.6 convolution_reduce_fusion
  516.5 68.5 %all-gather.5 = f32[131072]{0:T(1024)S(1)} all-gather(f32[4096]{0:T(1024)S(1)} %convolution_reduce_fusion), channel_id=7, replica_groups=mesh['grp'=4,'mem'=8] {'grp','mem'}, dimensions={0}, use_global_device_ids=true | all-gather | bytes 540672 | tf_op jit(solution)/shard_map/all_gather | solution.py:45
  588.4 5.7 convolution_reduce_fusion.8
  594.3 3.3 scatter_custom_fusion
  598.6 3.7 all-to-all-start
  602.4 6.4 scatter_custom_fusion.1
  609.0 5.8 all-to-all-start.1
  617.4 20.6 %all-to-all-done.1 = bf16[8,256,256]{2,1,0:T(8,128)(2,1)S(1)} async-done(((bf16[8,256,256]{2,1,0:T(8,128)(2,1)}), bf16[8,256,256]{2,1,0:T(8,128)(2,1)S(1)}, u32[]{:S(2)}, u32[]{:S(2)}) %all-to-all-start.1) | async-done | bytes 1048608 | tf_op jit(solution)/shard_map/all_to_all | solution.py:109
  639.1 19.9 %while.11 = (s32[]{:T(128)}, f32[8,256,256]{1,2,0:T(8,128)}, f32[8,2048]{1,0:T(8,128)S(1)}, f32[2048]{0:T(1024)S(1)}, f32[2048,256]{1,0:T(8,128)S(1)}, /*index=5*/bf16[2048,256]{1,0:T(8,128)(2,1)S(1)}, s32[]{:T(128)}) while((s32[]{:T(128)}, f32[8,256,256]{1,2,0:T(8,128)}, f32[8,2048]{1,0:T(8,128)S(1)}, f32[2048]{0:T(1024)S(1)}, ...), condition=%wide.region_40.41_spmd, body=%wide.region_39.40_spmd.sunk | while | flops 540084224 | bytes 10281053 | solution.py:62
  649.9 1.6 fusion.185
  652.4 1.6 fusion.185
  659.0 3.1 broadcast_add_fusion
  662.1 3.0 copy.34
  665.1 1.9 fusion.4
  668.4 94.4 %custom-call.20 = f32[8,128,128]{2,1,0:T(8,128)} custom-call(f32[8,128,128]{2,1,0:T(8,128)S(1)} %cholesky.119), custom_call_target="Cholesky" | custom-call | tf_op jit(solution)/shard_map/jit(cholesky)/cholesky | solution.py:67
  765.0 80.0 %custom-call.21 = f32[8,1,128,128]{2,3,1,0:T(8,128)} custom-call(f32[8,1,128,128]{3,2,1,0:T(8,128)} %select_bitcast_fusion), custom_call_target="InvertDiagBlocksLowerTriangular" | custom-call | tf_op jit(solution)/shard_map/jit(cholesky)/cholesky | solution.py:67
  845.1 1.9 constant_dynamic-update-slice_fusion.1
  847.0 3.1 convolution_subtract_fusion
  850.0 95.4 %custom-call.22 = f32[8,128,128]{2,1,0:T(8,128)} custom-call(f32[8,128,128]{2,1,0:T(8,128)} %convolution_subtract_fusion), custom_call_target="Cholesky" | custom-call | tf_op jit(solution)/shard_map/jit(cholesky)/cholesky | solution.py:67
  948.4 1.9 select_select_fusion
  950.4 5.9 while.12
  951.1 2.3 bitcast_dynamic-update-slice_fusion.2
  954.1 2.3 bitcast_dynamic-update-slice_fusion.2
  956.4 158.7 %custom-call.23 = f32[8,2,128,128]{2,3,1,0:T(8,128)} custom-call(f32[8,2,128,128]{3,2,1,0:T(8,128)} %bitcast.163), custom_call_target="InvertDiagBlocksLowerTriangular" | custom-call | tf_op jit(solution)/shard_map/jit(_cho_solve)/vmap()/triangular_solve | solution.py:68
  1115.0 1.7 fusion.15
  1119.2 2.0 fusion.16
  1123.5 9.7 all_to_all.33
  1133.3 10.5 gather_fusion
  (226 shorter events, 46.2 us)
Async XLA Ops:
  1.4 5.9 copy-start.12
  1.4 5.9 copy-start.19
  1.4 5.9 copy-start
  7.4 43.3 %copy-start.4 = (f32[4096]{0:T(1024)S(1)}, f32[4096]{0:T(1024)}, u32[]{:S(2)}) copy-start(f32[4096]{0:T(1024)} %param.16) | copy-start | bytes 49156
  7.4 43.3 %copy-start.8 = (f32[4096]{0:T(1024)S(1)}, f32[4096]{0:T(1024)}, u32[]{:S(2)}) copy-start(f32[4096]{0:T(1024)} %param.17) | copy-start | bytes 49156
  50.8 5.9 copy-start.1
  516.5 71.3 %copy-start.23 = (s32[1024]{0:T(1024)S(1)}, s32[1024]{0:T(1024)}, u32[]{:S(2)}) copy-start(s32[1024]{0:T(1024)} %param.13) | copy-start | bytes 12292
  516.5 71.9 %copy-start.24 = (s32[1024]{0:T(1024)S(1)}, s32[1024]{0:T(1024)}, u32[]{:S(2)}) copy-start(s32[1024]{0:T(1024)} %param.12) | copy-start | bytes 12292
  598.6 10.4 all-to-all-start
  609.0 29.0 %all-to-all-start.1 = ((bf16[8,256,256]{2,1,0:T(8,128)(2,1)}), bf16[8,256,256]{2,1,0:T(8,128)(2,1)S(1)}, u32[]{:S(2)}, u32[]{:S(2)}) async-start(bf16[8,256,256]{2,1,0:T(8,128)(2,1)} %bitcast.10), calls=%async_computation.1 | async-start | bytes 2097152 | tf_op jit(solution)/shard_map/all_to_all | solution.py:109
  614.8 23.2 %copy-start.21 = (f32[8]{0:T(128)}, f32[8]{0:T(128)S(1)}, u32[]{:S(2)}) copy-start(f32[8]{0:T(128)S(1)} %iota_convert_fusion) | copy-start | bytes 100
  616.6 21.4 %copy-start.9 = (f32[1,8,256]{2,0,1:T(1,128)}, f32[1,8,256]{2,0,1:T(1,128)S(1)}, u32[]{:S(2)}) copy-start(f32[1,8,256]{2,0,1:T(1,128)S(1)} %get-tuple-element.123) | copy-start | bytes 24580
  662.1 3.0 copy-start.2
  667.0 1.4 copy-start.5
  668.4 95.8 %copy-start.14 = (pred[128,128]{1,0:T(8,128)(4,1)S(1)}, pred[128,128]{1,0:T(8,128)(4,1)}, u32[]{:S(2)}) copy-start(pred[128,128]{1,0:T(8,128)(4,1)} %iota_compare_fusion.2) | copy-start | bytes 49156
  762.9 1.3 copy-start.6
  845.1 100.4 %copy-start.10 = (f32[1,8,256]{2,0,1:T(1,128)S(1)}, f32[1,8,256]{2,0,1:T(1,128)}, u32[]{:S(2)}) copy-start(f32[1,8,256]{2,0,1:T(1,128)} %copy-done.9) | copy-start | bytes 24580
  845.1 100.4 %copy-start.11 = (bf16[2048,8]{0,1:T(8,128)(2,1)S(1)}, bf16[2048,8]{0,1:T(8,128)(2,1)}, u32[]{:S(2)}) copy-start(bf16[2048,8]{0,1:T(8,128)(2,1)} %select_convert_fusion) | copy-start | bytes 98308
  845.1 100.4 %copy-start.15 = (f32[8,256]{1,0:T(8,128)S(1)}, f32[8,256]{1,0:T(8,128)}, u32[]{:S(2)}) copy-start(f32[8,256]{1,0:T(8,128)} %fusion.128) | copy-start | bytes 24580
  845.1 100.4 %copy-start.22 = (f32[8]{0:T(128)S(1)}, f32[8]{0:T(128)}, u32[]{:S(2)}) copy-start(f32[8]{0:T(128)} %copy-done.21) | copy-start | bytes 100
  847.0 98.8 %copy-start.13 = (pred[128,128]{1,0:T(8,128)(4,1)S(1)}, pred[128,128]{1,0:T(8,128)(4,1)}, u32[]{:S(2)}) copy-start(pred[128,128]{1,0:T(8,128)(4,1)} %iota_compare_fusion.3) | copy-start | bytes 49156
  945.7 4.6 copy-start.16
  947.1 1.4 copy-start.3
  948.4 1.9 copy-start.25
  950.4 164.6 %slice-start = ((f32[8,256,1]{1,0,2:T(8,128)}), f32[8,128,1]{1,0,2:T(8,128)S(1)}, s32[]{:S(2)}) async-start(f32[8,256,1]{1,0,2:T(8,128)} %copy-done.16), calls=%async_computation.3 | async-start | bytes 8192 | tf_op jit(solution)/shard_map/jit(_cho_solve)/vmap()/triangular_solve | solution.py:68
  950.4 167.2 %copy-start.17 = (f32[8,256,1]{1,0,2:T(8,128)S(1)}, f32[8,256,1]{1,0,2:T(8,128)}, u32[]{:S(2)}) copy-start(f32[8,256,1]{1,0,2:T(8,128)} %copy-done.16) | copy-start | bytes 24580
  1115.0 6.8 copy-start.7
  1119.2 14.0 %copy-start.20 = (s32[1024]{0:T(1024)S(1)}, s32[1024]{0:T(1024)}, u32[]{:S(2)}) copy-start(s32[1024]{0:T(1024)} %get-tuple-element.126) | copy-start | bytes 12292
  1122.7 21.1 %copy-start.18 = (f32[8,256]{1,0:T(8,128)}, f32[8,256]{1,0:T(8,128)S(1)}, u32[]{:S(2)}) copy-start(f32[8,256]{1,0:T(8,128)S(1)} %get-tuple-element.95) | copy-start | bytes 24580
